TPU v7x, 256 devices: a whole 4x4x8 slice. The times are simulated.
256 devices in a mesh: gx: 8 (over z), gy: 32 (over y, x, core).
Axes of the slice: x: 4, y: 4, z: 8, core: 2. Of those that a mesh axis runs over, the one named last changes fastest.
Arguments:
- child_coef: bfloat16 [512, 16, 128, 128], P(('gx', 'gy')), may hold values from -6 to 6
- transfer: bfloat16 [512, 64, 2, 128, 128], P(('gx', 'gy')), may hold values from -0.125 to 0.125
- child_dir: int32 [512, 64], P(('gx', 'gy')), may hold values from 0 to 15, as said below
- couple_src: int32 [64, 64, 7], P('gx', 'gy'), may hold values from 0 to 63, as said below
- couple_kind: int32 [64, 64, 7], P('gx', 'gy'), may hold values from 0 to 7
- couple_count: int32 [64, 64], P('gx', 'gy'), may hold values from 1 to 7, as said below
- couple_table: bfloat16 [64, 8, 2, 128, 128], P('gy'), may hold values from -0.1875 to 0.1875
Outputs:
- child_local: bfloat16 [512, 16, 128, 128], P(('gx', 'gy'))
Inputs may be any that keep to these rules, and one draw needn't show every extreme that they name: `child_dir`: in every row each child direction is named by exactly four parent directions. `couple_src`: the entries of one block row are distinct and never the row's own parent cluster. `couple_count`: some row holds 7.
All inputs are finite; a program needn't handle non-finite values.
Results may differ from a plain program's by a relative error of at most 0.015.
Values may be sent and summed in bfloat16 or wider, within the bound.
A program may use at most 128 MiB of HBM per device.

v0:
```python
import jax
import jax.numpy as jnp
from jax import lax
from jax.sharding import PartitionSpec as P

CPD = 2


def complex_apply(real_part, imag_part, vectors, pattern):
    halfway = vectors.shape[-1] // 2
    real_term = jnp.einsum(pattern, real_part, vectors, preferred_element_type=jnp.float32)
    imag_term = jnp.einsum(pattern, imag_part, vectors, preferred_element_type=jnp.float32)
    return jnp.concatenate(
        [
            real_term[..., :halfway] - imag_term[..., halfway:],
            real_term[..., halfway:] + imag_term[..., :halfway],
        ],
        axis=-1,
    )


def sum_groups(received):
    groups = received.shape[0] // (8 // CPD)
    merged = received.astype(jnp.float32).reshape((groups, 8 // CPD) + received.shape[1:])
    return jnp.sum(merged, axis=1).astype(jnp.bfloat16)


def body(child_coef, transfer, child_dir, couple_src, couple_kind, couple_count, couple_table):
    picked = jnp.take_along_axis(child_coef, child_dir[:, :, None, None], axis=1)
    upward = complex_apply(transfer[:, :, 0], transfer[:, :, 1], picked, "cers,cesa->cera")
    summed = jnp.sum(upward, axis=0, keepdims=True).astype(jnp.bfloat16)
    parent = sum_groups(lax.all_to_all(summed, "gy", split_axis=1, concat_axis=0, tiled=True))
    everything = lax.all_gather(parent, "gx", axis=0, tiled=True)
    dir_local = jnp.arange(parent.shape[1], dtype=jnp.int32)[None, :, None]
    sources = everything[couple_src, dir_local]
    matrices = couple_table[dir_local, couple_kind]
    products = complex_apply(
        matrices[:, :, :, 0], matrices[:, :, :, 1], sources, "uemrs,uemsa->uemra"
    )
    active = jnp.arange(couple_src.shape[-1], dtype=jnp.int32) < couple_count[..., None]
    parent_local = jnp.sum(jnp.where(active[..., None, None], products, 0.0), axis=2).astype(
        jnp.bfloat16
    )
    copies = jnp.repeat(parent_local, 8 // CPD, axis=0)
    parent_row = lax.all_to_all(copies, "gy", split_axis=0, concat_axis=1, tiled=True)[0]
    descent = complex_apply(transfer[:, :, 0], transfer[:, :, 1], parent_row, "cesr,esa->cera")
    child_index = jnp.arange(child_coef.shape[1], dtype=jnp.int32)
    onehot = (child_dir[:, None, :] == child_index[None, :, None]).astype(jnp.float32)
    child_local = jnp.einsum("cie,cera->cira", onehot, descent)
    return child_local.astype(jnp.bfloat16)


def solution(mesh):
    return jax.shard_map(
        body,
        mesh=mesh,
        in_specs=(
            P(("gx", "gy"), None, None, None),
            P(("gx", "gy"), None, None, None, None),
            P(("gx", "gy"), None),
            P("gx", "gy", None),
            P("gx", "gy", None),
            P("gx", "gy"),
            P("gy", None, None, None, None),
        ),
        out_specs=P(("gx", "gy"), None, None, None),
        check_vma=False,
    )
```

profile of v0, /device:TPU:1, one launch (start us, length us, event | category | flops | bytes accessed | tf_op | source)
XLA Modules:
  0.0 241.7 jit_solution(4865288829287410528)
XLA Ops:
  6.5 0.0 copy-start
  6.5 0.0 all-gather.2.cloned.1.call-start
  6.5 0.8 bitcast_or_fusion
  7.3 0.7 compare_and_fusion
  8.0 0.1 reshape.63
  8.1 4.3 %gather_fusion.2 = bf16[128,128,128]{2,1,0:T(8,128)(2,1)} fusion(bf16[2,16,128,128]{3,2,1,0:T(8,128)(2,1)} %param.7, s32[128]{0:T(128)S(1)} %reshape.63), kind=kCustom, calls=%fused_computation.2 | custom fusion | bytes 8389632 | tf_op jit(solution)/shard_map/jit(take_along_axis)/gather | solution.py:29
  12.4 6.3 %copy.35 = bf16[2,64,128,128]{2,3,1,0:T(8,128)(2,1)} copy(bf16[2,64,128,128]{3,2,1,0:T(8,128)(2,1)} %bitcast.69) | data formatting | bytes 8388608 | tf_op jit(solution)/shard_map/jit(take_along_axis)/gather | solution.py:29
  18.7 0.0 copy-start.2
  18.7 9.9 %fusion.10 = f32[2,64,128,128]{2,3,1,0:T(8,128)} fusion(bf16[2,64,128,128]{2,3,1,0:T(8,128)(2,1)} %copy.35, pred[2,64]{1,0:T(4,128)(4,1)S(1)} %compare_and_fusion, bf16[2,64,2,128,128]{4,3,2,1,0:T(8,128)(2,1)} %param.8), kind=kOutput, calls=%fused_computation.27 | convolution fusion | flops 538968064 | bytes 16777344 | tf_op jit(solution)/shard_map/cers,cesa->cera/dot_general | solution.py:12
  28.6 0.0 copy-done.2
  28.6 8.5 %fusion.9 = f32[2,64,128,128]{2,3,1,0:T(8,128)} fusion(bf16[2,64,128,128]{2,3,1,0:T(8,128)(2,1)S(1)} %copy-done.2, pred[2,64]{1,0:T(4,128)(4,1)S(1)} %compare_and_fusion, bf16[2,64,2,128,128]{4,3,2,1,0:T(8,128)(2,1)} %param.8), kind=kOutput, calls=%fused_computation.26 | convolution fusion | flops 538968064 | bytes 16777344 | tf_op jit(solution)/shard_map/cers,cesa->cera/dot_general | solution.py:11
  37.1 10.3 %slice_subtract_fusion.1 = (f32[2,64,128,64]{2,3,1,0:T(8,128)S(1)}, f32[2,64,128,64]{2,3,1,0:T(8,128)}) fusion(f32[2,64,128,128]{2,3,1,0:T(8,128)} %fusion.10, f32[2,64,128,128]{2,3,1,0:T(8,128)} %fusion.9), kind=kLoop, calls=%fused_computation.10 | loop fusion | flops 2097152 | bytes 25165824 | tf_op jit(solution)/shard_map/sub | solution.py:15
  47.5 5.0 %maximum_reduce_fusion = bf16[64,128,128]{1,2,0:T(8,128)(2,1)} fusion(f32[2,64,128,64]{2,3,1,0:T(8,128)} %get-tuple-element.8, f32[2,64,128,64]{2,3,1,0:T(8,128)S(1)} %get-tuple-element.7), kind=kLoop, calls=%fused_computation.3 | loop fusion | flops 3145728 | bytes 10485760 | tf_op jit(solution)/shard_map/reduce_sum | solution.py:31
  52.4 4.1 %copy.38 = bf16[1,64,128,128]{3,2,0,1:T(8,128)(2,1)} copy(bf16[1,64,128,128]{2,3,1,0:T(8,128)(2,1)} %bitcast.70) | data formatting | bytes 4194304 | tf_op jit(solution)/shard_map/convert_element_type | solution.py:31
  56.5 0.0 copy-start.7
  56.5 0.0 copy-start.8
  56.5 37.0 %all_to_all.21 = bf16[1,64,128,128]{3,2,0,1:T(8,128)(2,1)S(1)} all-to-all(bf16[1,64,128,128]{3,2,0,1:T(8,128)(2,1)} %copy.38), channel_id=1, replica_groups=mesh['gx'=8,'gy'=32] {'gy'}, dimensions={1} | all-to-all | bytes 4194304 | tf_op jit(solution)/shard_map/all_to_all | solution.py:32
  93.5 1.3 reduce_sum.31
  94.8 0.0 all-gather.2.cloned.1.call-update
  94.8 0.0 copy-done.7
  94.9 0.1 copy.39
  94.9 0.1 reshape.57
  95.0 0.0 copy-done.8
  95.1 0.1 copy.33
  95.2 0.1 reshape.51
  95.3 0.0 copy-done
  95.3 7.8 %gather_fusion = bf16[112,2,128,128]{3,2,1,0:T(8,128)(2,1)} fusion(bf16[2,8,2,128,128]{4,3,2,1,0:T(8,128)(2,1)S(1)} %copy-done, s32[112]{0:T(128)S(1)} %reshape.51), kind=kCustom, calls=%fused_computation | custom fusion | bytes 14680960 | tf_op jit(solution)/shard_map/gather | solution.py:36
  103.1 0.0 copy-start.9
  103.1 9.4 %copy.34 = bf16[112,2,128,128]{3,2,0,1:T(8,128)(2,1)} copy(bf16[112,2,128,128]{3,2,1,0:T(8,128)(2,1)} %gather_fusion) | data formatting | bytes 14680064 | tf_op jit(solution)/shard_map/gather | solution.py:36
  112.5 0.0 copy-done.9
  112.5 0.1 copy.32
  112.6 0.1 iota_compare_fusion.1
  112.6 36.0 %all-gather.2.cloned.1.call-done = bf16[64,2,128,128]{3,2,1,0:T(8,128)(2,1)} async-done(((bf16[8,2,128,128]{3,2,1,0:T(8,128)(2,1)}), bf16[64,2,128,128]{3,2,1,0:T(8,128)(2,1)}) %all-gather.2.cloned.1.call-update) | async-done | bytes 4194320 | tf_op jit(solution)/shard_map/all_gather | solution.py:33
  148.6 5.5 %gather_fusion.1 = bf16[112,128,128]{2,1,0:T(8,128)(2,1)} fusion(bf16[64,2,128,128]{3,2,1,0:T(8,128)(2,1)} %all-gather.2.cloned.1.call-done, s32[112]{0:T(128)S(1)} %reshape.57), kind=kCustom, calls=%fused_computation.1 | custom fusion | bytes 7340928 | tf_op jit(solution)/shard_map/gather | solution.py:35
  154.1 0.0 copy-start.3
  154.1 0.0 copy-start.4
  154.1 6.0 %fusion.7 = f32[8,2,7,128,128]{3,4,2,1,0:T(8,128)S(1)} fusion(bf16[8,2,7,128,128]{4,3,2,1,0:T(8,128)(2,1)} %bitcast.63, bf16[8,2,7,2,128,128]{5,4,2,1,0,3:T(8,128)(2,1)} %bitcast.65), kind=kOutput, calls=%fused_computation.23 | convolution fusion | flops 469762048 | bytes 14680064 | tf_op jit(solution)/shard_map/uemrs,uemsa->uemra/dot_general | solution.py:12
  160.1 0.0 copy-done.3
  160.1 0.3 copy-done.4
  160.5 5.6 %fusion.8 = f32[8,2,7,128,128]{3,4,2,1,0:T(8,128)} fusion(bf16[8,2,7,128,128]{4,3,2,1,0:T(8,128)(2,1)S(1)} %bitcast.64, bf16[8,2,7,2,128,128]{5,4,2,1,0,3:T(8,128)(2,1)S(1)} %bitcast.66), kind=kOutput, calls=%fused_computation.25 | convolution fusion | flops 469762048 | bytes 14680064 | tf_op jit(solution)/shard_map/uemrs,uemsa->uemra/dot_general | solution.py:11
  166.1 7.7 %slice_subtract_fusion.2 = (f32[8,2,7,128,64]{3,4,2,1,0:T(8,128)S(1)}, f32[8,2,7,128,64]{3,4,2,1,0:T(8,128)}) fusion(f32[8,2,7,128,128]{3,4,2,1,0:T(8,128)S(1)} %fusion.7, f32[8,2,7,128,128]{3,4,2,1,0:T(8,128)} %fusion.8), kind=kLoop, calls=%fused_computation.21 | loop fusion | flops 1835008 | bytes 22020096 | tf_op jit(solution)/shard_map/sub | solution.py:15
  173.8 2.8 %fusion = bf16[8,2,128,128]{2,3,1,0:T(8,128)(2,1)S(1)} fusion(f32[8,2,7,128,64]{3,4,2,1,0:T(8,128)} %get-tuple-element.10, f32[8,2,7,128,64]{3,4,2,1,0:T(8,128)S(1)} %get-tuple-element.9, pred[8,2,7]{2,1,0:T(4,128)(4,1)S(1)} %iota_compare_fusion.1), kind=kLoop, calls=%fused_computation.6 | loop fusion | flops 5242880 | bytes 7864432 | tf_op jit(solution)/shard_map/reduce_sum | solution.py:41
  176.6 1.9 broadcast_in_dim.55
  178.5 7.7 %all-to-all-start.1 = ((bf16[32,2,128,128]{2,3,1,0:T(8,128)(2,1)}), bf16[32,2,128,128]{2,3,1,0:T(8,128)(2,1)S(1)}, u32[]{:S(2)}, u32[]{:S(2)}) async-start(bf16[32,2,128,128]{2,3,1,0:T(8,128)(2,1)} %bitcast.71), calls=%async_computation.1 | async-start | bytes 4194304 | tf_op jit(solution)/shard_map/all_to_all | solution.py:45
  186.2 6.1 %slice_bitcast_fusion.1 = (bf16[2,64,128,128]{3,2,1,0:T(8,128)(2,1)}, bf16[2,64,128,128]{3,2,1,0:T(8,128)(2,1)}) fusion(bf16[2,64,2,128,128]{4,3,2,1,0:T(8,128)(2,1)} %param.8), kind=kLoop, calls=%fused_computation.16 | loop fusion | bytes 16777216 | tf_op jit(solution)/shard_map/squeeze | solution.py:30
  192.3 22.5 %all-to-all-done.1 = bf16[32,2,128,128]{2,3,1,0:T(8,128)(2,1)S(1)} async-done(((bf16[32,2,128,128]{2,3,1,0:T(8,128)(2,1)}), bf16[32,2,128,128]{2,3,1,0:T(8,128)(2,1)S(1)}, u32[]{:S(2)}, u32[]{:S(2)}) %all-to-all-start.1) | async-done | bytes 2097184 | tf_op jit(solution)/shard_map/all_to_all | solution.py:45
  214.8 0.0 copy-start.5
  214.8 3.6 %fusion.11 = f32[2,64,128,128]{2,3,0,1:T(8,128)S(1)} fusion(bf16[64,128,128,1]{1,2,3,0:T(8,128)(2,1)S(1)} %bitcast.67, bf16[2,64,128,128]{3,2,1,0:T(8,128)(2,1)} %get-tuple-element.11), kind=kOutput, calls=%fused_computation.28 | convolution fusion | flops 536870912 | bytes 14680064 | tf_op jit(solution)/shard_map/cesr,esa->cera/dot_general | solution.py:11
  218.4 0.0 copy-done.5
  218.4 1.2 fusion.14
  219.7 2.1 slice_subtract_fusion
  221.8 2.3 pad_maximum_fusion
  224.0 0.0 copy-start.6
  224.0 0.0 copy-start.1
  224.0 6.7 %copy.44 = bf16[2,64,128,128]{3,1,2,0:T(8,128)(2,1)} copy(bf16[2,64,128,128]{2,3,0,1:T(8,128)(2,1)} %pad_maximum_fusion) | data formatting | bytes 8388608 | tf_op jit(solution)/shard_map/concatenate | solution.py:13
  230.7 0.0 copy-done.6
  230.7 2.8 %convolution_convert_fusion = bf16[2,16,128,128]{3,1,2,0:T(8,128)(2,1)S(1)} fusion(bf16[2,64,128,128]{3,1,2,0:T(8,128)(2,1)} %copy.44, s32[2,64]{1,0:T(2,128)S(1)} %copy-done.6), kind=kOutput, calls=%fused_computation.33 | convolution fusion | flops 67110912 | bytes 5243392 | tf_op jit(solution)/shard_map/cie,cera->cira/dot_general | solution.py:49
  233.6 1.2 copy.45
  234.8 0.0 copy-done.1
  (2 shorter events, 0.0 us)
Async XLA Ops:
  6.5 88.7 %copy-start = (bf16[2,8,2,128,128]{4,3,2,1,0:T(8,128)(2,1)S(1)}, bf16[2,8,2,128,128]{4,3,2,1,0:T(8,128)(2,1)}, u32[]{:S(2)}) copy-start(bf16[2,8,2,128,128]{4,3,2,1,0:T(8,128)(2,1)} %param.13) | copy-start | bytes 3145732
  6.5 142.1 %all-gather.2.cloned.1.call-start = ((), (), s32[]{:S(2)}) async-start(), calls=%async_computation.2 | async-start | bytes 4718592 | tf_op jit(solution)/shard_map/all_gather | solution.py:33
  18.7 9.9 %copy-start.2 = (bf16[2,64,128,128]{2,3,1,0:T(8,128)(2,1)S(1)}, bf16[2,64,128,128]{2,3,1,0:T(8,128)(2,1)}, u32[]{:S(2)}) copy-start(bf16[2,64,128,128]{2,3,1,0:T(8,128)(2,1)} %copy.35) | copy-start | bytes 12582916
  56.5 38.3 %copy-start.7 = (s32[8,2,7]{0,1,2:T(2,128)S(1)}, s32[8,2,7]{0,1,2:T(2,128)}, u32[]{:S(2)}) copy-start(s32[8,2,7]{0,1,2:T(2,128)} %param.10) | copy-start | bytes 1348
  56.5 38.6 %copy-start.8 = (s32[8,2,7]{0,1,2:T(2,128)S(1)}, s32[8,2,7]{0,1,2:T(2,128)}, u32[]{:S(2)}) copy-start(s32[8,2,7]{0,1,2:T(2,128)} %param.11) | copy-start | bytes 1348
  103.1 9.4 %copy-start.9 = (s32[8,2]{0,1:T(2,128)S(1)}, s32[8,2]{0,1:T(2,128)}, u32[]{:S(2)}) copy-start(s32[8,2]{0,1:T(2,128)} %param.12) | copy-start | bytes 196
  154.1 6.0 %copy-start.3 = (bf16[112,128,128]{2,1,0:T(8,128)(2,1)S(1)}, bf16[112,128,128]{2,1,0:T(8,128)(2,1)}, u32[]{:S(2)}) copy-start(bf16[112,128,128]{2,1,0:T(8,128)(2,1)} %gather_fusion.1) | copy-start | bytes 11010052
  154.1 6.3 %copy-start.4 = (bf16[112,2,128,128]{3,2,0,1:T(8,128)(2,1)S(1)}, bf16[112,2,128,128]{3,2,0,1:T(8,128)(2,1)}, u32[]{:S(2)}) copy-start(bf16[112,2,128,128]{3,2,0,1:T(8,128)(2,1)} %copy.34) | copy-start | bytes 22020100
  178.5 36.3 %all-to-all-start.1 = ((bf16[32,2,128,128]{2,3,1,0:T(8,128)(2,1)}), bf16[32,2,128,128]{2,3,1,0:T(8,128)(2,1)S(1)}, u32[]{:S(2)}, u32[]{:S(2)}) async-start(bf16[32,2,128,128]{2,3,1,0:T(8,128)(2,1)} %bitcast.71), calls=%async_computation.1 | async-start | bytes 4194304 | tf_op jit(solution)/shard_map/all_to_all | solution.py:45
  214.8 3.6 %copy-start.5 = (bf16[2,64,128,128]{3,2,1,0:T(8,128)(2,1)S(1)}, bf16[2,64,128,128]{3,2,1,0:T(8,128)(2,1)}, u32[]{:S(2)}) copy-start(bf16[2,64,128,128]{3,2,1,0:T(8,128)(2,1)} %get-tuple-element.12) | copy-start | bytes 12582916
  224.0 6.7 %copy-start.6 = (s32[2,64]{1,0:T(2,128)S(1)}, s32[2,64]{1,0:T(2,128)}, u32[]{:S(2)}) copy-start(s32[2,64]{1,0:T(2,128)} %param.9) | copy-start | bytes 1540
  224.0 10.8 %copy-start.1 = (bf16[2,8,2,128,128]{4,3,2,1,0:T(8,128)(2,1)S(1)}, bf16[2,8,2,128,128]{4,3,2,1,0:T(8,128)(2,1)}, u32[]{:S(2)}) copy-start(bf16[2,8,2,128,128]{4,3,2,1,0:T(8,128)(2,1)} %param.13) | copy-start | bytes 3145732
Sparse Core Ops, SparseCore 0:
  94.9 53.6 all-gather.1
where the time goes:
time: 242 us
  waiting for transfers between devices  58.5 us (24%)
  local copies, waits for them, and re-layouts  54.2 us (22%)
  matrix products  37.7 us (16%)
  blocking collectives  37 us (15%)
  other arithmetic  33 us (14%)
  between operations  13.5 us (6%)
  starting transfers between devices  7.7 us (3%)
    all_to_all x1, blocking collectives, body(): lax.all_to_all(summed, 'gy', split_axis=1, concat_axis=0, tiled=True)  37 us
    all_gather x1, waiting for transfers between devices, body(): everything = lax.all_gather(parent, 'gx', axis=0, tiled=True)  36 us
    all_to_all x1, waiting for transfers between devices, body(): lax.all_to_all(copies, 'gy', split_axis=0, concat_axis=1, tiled=True)[0]  22.5 us
    sub x3, other arithmetic, complex_apply(): real_term[..., :halfway] - imag_term[..., halfway:]  20.1 us
    dot_general x3, matrix products, complex_apply(): jnp.einsum(pattern, real_part, vectors, preferred_element_type=jnp.float32)  17.7 us
    gather x2, local copies, waits for them, and re-layouts, body(): matrices = couple_table[dir_local, couple_kind]  17.2 us
    dot_general x3, matrix products, complex_apply(): jnp.einsum(pattern, imag_part, vectors, preferred_element_type=jnp.float32)  17.2 us
    gather x3, local copies, waits for them, and re-layouts, body(): jnp.take_along_axis(child_coef, child_dir[:, :, None, None], axis=1)  10.7 us
  transfers between devices with their start and end apart: 2, of which 2 were waited for; matrix products, arithmetic and copies ran while one was open for 10% of the time, Pallas kernels for 0%

commit v1 on v0

--- a/solution.py
+++ b/solution.py
@@ -2,6 +2,7 @@
 import jax.numpy as jnp
 from jax import lax
 from jax.sharding import PartitionSpec as P
+from jax.lax import all_to_all, psum
 
 CPD = 2
 
@@ -30,7 +31,14 @@
     upward = complex_apply(transfer[:, :, 0], transfer[:, :, 1], picked, "cers,cesa->cera")
     summed = jnp.sum(upward, axis=0, keepdims=True).astype(jnp.bfloat16)
     parent = sum_groups(lax.all_to_all(summed, "gy", split_axis=1, concat_axis=0, tiled=True))
-    everything = lax.all_gather(parent, "gx", axis=0, tiled=True)
+
+    def start_circles(buf):
+        prior = psum(1, "gx")
+        x_now = jnp.stack(prior * [buf])
+        carry_in = all_to_all(x_now, "gx", 0, 0)
+        return jnp.concatenate(carry_in, axis=0)
+
+    everything = start_circles(parent)
     dir_local = jnp.arange(parent.shape[1], dtype=jnp.int32)[None, :, None]
     sources = everything[couple_src, dir_local]
     matrices = couple_table[dir_local, couple_kind]

time: 242 us -> 281 us (1.16)
  waiting for transfers between devices: 58.5 us -> 102 us
  between operations: 13.5 us -> 0.11 us
  starting transfers between devices: 7.7 us -> 12.8 us
  local copies, waits for them, and re-layouts: 54.2 us -> 58.2 us
    all_to_all x0 -> x1, waiting for transfers between devices: none -> 79.2 us  [start_circles(): carry_in = all_to_all(x_now, 'gx', 0, 0)]
    all_gather x1 -> x0, waiting for transfers between devices: 36 us -> none  [body(): everything = lax.all_gather(parent, 'gx', axis=0, tiled=True)]
    all_to_all x0 -> x1, starting transfers between devices: none -> 8.33 us  [start_circles(): carry_in = all_to_all(x_now, 'gx', 0, 0)]
    another operation x0 -> x1, local copies, waits for them, and re-layouts: none -> 4.13 us  [start_circles(): x_now = jnp.stack(prior * [buf])]
    all_to_all x1, starting transfers between devices: 7.7 us -> 4.45 us  [body(): lax.all_to_all(copies, 'gy', split_axis=0, concat_axis=1, tiled=True)[0]]
  transfers between devices with their start and end apart: 2 -> 2, of which waited for: 2 -> 2; matrix products, arithmetic and copies ran while one was open for 10% -> 8% of each run, Pallas kernels for 0% -> 0%
where the time goes in v1:
time: 281 us; the launch traced here: 280 us
  waiting for transfers between devices  102 us (36%)
  local copies, waits for them, and re-layouts  58.2 us (21%)
  matrix products  37.7 us (13%)
  blocking collectives  36.8 us (13%)
  other arithmetic  32.8 us (12%)
  starting transfers between devices  12.8 us (5%)
    all_to_all x1, waiting for transfers between devices, start_circles(): carry_in = all_to_all(x_now, 'gx', 0, 0)  79.2 us
    all_to_all x1, blocking collectives, body(): lax.all_to_all(summed, 'gy', split_axis=1, concat_axis=0, tiled=True)  36.8 us
    all_to_all x1, waiting for transfers between devices, body(): lax.all_to_all(copies, 'gy', split_axis=0, concat_axis=1, tiled=True)[0]  22.6 us
    sub x3, other arithmetic, complex_apply(): real_term[..., :halfway] - imag_term[..., halfway:]  20.1 us
    dot_general x3, matrix products, complex_apply(): jnp.einsum(pattern, real_part, vectors, preferred_element_type=jnp.float32)  17.7 us
    dot_general x3, matrix products, complex_apply(): jnp.einsum(pattern, imag_part, vectors, preferred_element_type=jnp.float32)  17.2 us
    gather x2, local copies, waits for them, and re-layouts, body(): matrices = couple_table[dir_local, couple_kind]  17 us
    gather x3, local copies, waits for them, and re-layouts, body(): jnp.take_along_axis(child_coef, child_dir[:, :, None, None], axis=1)  10.7 us
  transfers between devices with their start and end apart: 2, of which 2 were waited for; matrix products, arithmetic and copies ran while one was open for 8% of the time, Pallas kernels for 0%

profile of v1, /device:TPU:1, one launch (start us, length us, event | category | flops | bytes accessed | tf_op | source)
XLA Modules:
  0.0 280.2 jit_solution(12785140527498448354)
XLA Ops:
  0.0 0.0 copy-start
  0.0 0.8 bitcast_or_fusion
  0.8 0.7 compare_and_fusion
  1.5 0.1 reshape.69
  1.5 4.3 %gather_fusion.2 = bf16[128,128,128]{2,1,0:T(8,128)(2,1)} fusion(bf16[2,16,128,128]{3,2,1,0:T(8,128)(2,1)} %param.7, s32[128]{0:T(128)S(1)} %reshape.69), kind=kCustom, calls=%fused_computation.2 | custom fusion | bytes 8389632 | tf_op jit(solution)/shard_map/jit(take_along_axis)/gather | solution.py:30
  5.8 6.3 %copy.35 = bf16[2,64,128,128]{2,3,1,0:T(8,128)(2,1)} copy(bf16[2,64,128,128]{3,2,1,0:T(8,128)(2,1)} %bitcast.70) | data formatting | bytes 8388608 | tf_op jit(solution)/shard_map/jit(take_along_axis)/gather | solution.py:30
  12.2 0.0 copy-start.2
  12.2 9.9 %fusion.10 = f32[2,64,128,128]{2,3,1,0:T(8,128)} fusion(bf16[2,64,128,128]{2,3,1,0:T(8,128)(2,1)} %copy.35, pred[2,64]{1,0:T(4,128)(4,1)S(1)} %compare_and_fusion, bf16[2,64,2,128,128]{4,3,2,1,0:T(8,128)(2,1)} %param.8), kind=kOutput, calls=%fused_computation.27 | convolution fusion | flops 538968064 | bytes 16777344 | tf_op jit(solution)/shard_map/cers,cesa->cera/dot_general | solution.py:13
  22.1 0.0 copy-done.2
  22.1 8.5 %fusion.9 = f32[2,64,128,128]{2,3,1,0:T(8,128)} fusion(bf16[2,64,128,128]{2,3,1,0:T(8,128)(2,1)S(1)} %copy-done.2, pred[2,64]{1,0:T(4,128)(4,1)S(1)} %compare_and_fusion, bf16[2,64,2,128,128]{4,3,2,1,0:T(8,128)(2,1)} %param.8), kind=kOutput, calls=%fused_computation.26 | convolution fusion | flops 538968064 | bytes 16777344 | tf_op jit(solution)/shard_map/cers,cesa->cera/dot_general | solution.py:12
  30.6 10.3 %slice_subtract_fusion.1 = (f32[2,64,128,64]{2,3,1,0:T(8,128)S(1)}, f32[2,64,128,64]{2,3,1,0:T(8,128)}) fusion(f32[2,64,128,128]{2,3,1,0:T(8,128)} %fusion.10, f32[2,64,128,128]{2,3,1,0:T(8,128)} %fusion.9), kind=kLoop, calls=%fused_computation.10 | loop fusion | flops 2097152 | bytes 25165824 | tf_op jit(solution)/shard_map/sub | solution.py:16
  40.9 5.0 %maximum_reduce_fusion = bf16[64,128,128]{1,2,0:T(8,128)(2,1)} fusion(f32[2,64,128,64]{2,3,1,0:T(8,128)} %get-tuple-element.8, f32[2,64,128,64]{2,3,1,0:T(8,128)S(1)} %get-tuple-element.7), kind=kLoop, calls=%fused_computation.3 | loop fusion | flops 3145728 | bytes 10485760 | tf_op jit(solution)/shard_map/reduce_sum | solution.py:32
  45.9 4.1 %copy.38 = bf16[1,64,128,128]{3,2,0,1:T(8,128)(2,1)} copy(bf16[1,64,128,128]{2,3,1,0:T(8,128)(2,1)} %bitcast.71) | data formatting | bytes 4194304 | tf_op jit(solution)/shard_map/convert_element_type | solution.py:32
  49.9 36.8 %all_to_all.26 = bf16[1,64,128,128]{3,2,0,1:T(8,128)(2,1)S(1)} all-to-all(bf16[1,64,128,128]{3,2,0,1:T(8,128)(2,1)} %copy.38), channel_id=1, replica_groups=mesh['gx'=8,'gy'=32] {'gy'}, dimensions={1} | all-to-all | bytes 4194304 | tf_op jit(solution)/shard_map/all_to_all | solution.py:33
  86.8 1.3 reduce_sum.31
  88.1 4.1 %stack.2 = bf16[8,8,2,128,128]{4,3,2,1,0:T(8,128)(2,1)} broadcast(bf16[8,2,128,128]{3,2,1,0:T(8,128)(2,1)} %reduce_sum.31), dimensions={1,2,3,4} | broadcast | bytes 4718592 | tf_op jit(solution)/shard_map/stack | solution.py:37
  92.2 0.0 copy-start.7
  92.2 0.0 copy-start.8
  92.2 8.3 %all-to-all-start.1 = ((bf16[8,8,2,128,128]{4,3,2,1,0:T(8,128)(2,1)}), bf16[8,8,2,128,128]{4,3,2,1,0:T(8,128)(2,1)}, u32[]{:S(2)}, u32[]{:S(2)}) async-start(bf16[8,8,2,128,128]{4,3,2,1,0:T(8,128)(2,1)} %stack.2), calls=%async_computation.1 | async-start | bytes 8388608 | tf_op jit(solution)/shard_map/all_to_all | solution.py:38
  100.6 0.0 copy-done.7
  100.6 0.1 copy.39
  100.7 0.1 reshape.63
  100.8 0.0 copy-done.8
  100.8 0.1 copy.33
  100.9 0.1 reshape.57
  101.0 0.0 copy-done
  101.0 7.8 %gather_fusion = bf16[112,2,128,128]{3,2,1,0:T(8,128)(2,1)} fusion(bf16[2,8,2,128,128]{4,3,2,1,0:T(8,128)(2,1)S(1)} %copy-done, s32[112]{0:T(128)S(1)} %reshape.57), kind=kCustom, calls=%fused_computation | custom fusion | bytes 14680960 | tf_op jit(solution)/shard_map/gather | solution.py:44
  108.8 0.0 copy-start.9
  108.8 9.2 %copy.34 = bf16[112,2,128,128]{3,2,0,1:T(8,128)(2,1)} copy(bf16[112,2,128,128]{3,2,1,0:T(8,128)(2,1)} %gather_fusion) | data formatting | bytes 14680064 | tf_op jit(solution)/shard_map/gather | solution.py:44
  118.1 0.0 copy-done.9
  118.1 0.1 copy.32
  118.1 0.1 iota_compare_fusion.1
  118.2 79.2 %all-to-all-done.1 = bf16[8,8,2,128,128]{4,3,2,1,0:T(8,128)(2,1)} async-done(((bf16[8,8,2,128,128]{4,3,2,1,0:T(8,128)(2,1)}), bf16[8,8,2,128,128]{4,3,2,1,0:T(8,128)(2,1)}, u32[]{:S(2)}, u32[]{:S(2)}) %all-to-all-start.1) | async-done | bytes 4194336 | tf_op jit(solution)/shard_map/all_to_all | solution.py:38
  197.5 5.5 %gather_fusion.1 = bf16[112,128,128]{2,1,0:T(8,128)(2,1)} fusion(bf16[64,2,128,128]{3,2,1,0:T(8,128)(2,1)} %bitcast.13, s32[112]{0:T(128)S(1)} %reshape.63), kind=kCustom, calls=%fused_computation.1 | custom fusion | bytes 7340928 | tf_op jit(solution)/shard_map/gather | solution.py:43
  203.0 0.0 copy-start.3
  203.0 0.0 copy-start.4
  203.0 6.0 %fusion.7 = f32[8,2,7,128,128]{3,4,2,1,0:T(8,128)S(1)} fusion(bf16[8,2,7,128,128]{4,3,2,1,0:T(8,128)(2,1)} %bitcast.64, bf16[8,2,7,2,128,128]{5,4,2,1,0,3:T(8,128)(2,1)} %bitcast.66), kind=kOutput, calls=%fused_computation.23 | convolution fusion | flops 469762048 | bytes 14680064 | tf_op jit(solution)/shard_map/uemrs,uemsa->uemra/dot_general | solution.py:13
  209.0 0.0 copy-done.3
  209.0 0.3 copy-done.4
  209.3 5.6 %fusion.8 = f32[8,2,7,128,128]{3,4,2,1,0:T(8,128)} fusion(bf16[8,2,7,128,128]{4,3,2,1,0:T(8,128)(2,1)S(1)} %bitcast.65, bf16[8,2,7,2,128,128]{5,4,2,1,0,3:T(8,128)(2,1)S(1)} %bitcast.67), kind=kOutput, calls=%fused_computation.25 | convolution fusion | flops 469762048 | bytes 14680064 | tf_op jit(solution)/shard_map/uemrs,uemsa->uemra/dot_general | solution.py:12
  215.0 7.7 %slice_subtract_fusion.2 = (f32[8,2,7,128,64]{3,4,2,1,0:T(8,128)S(1)}, f32[8,2,7,128,64]{3,4,2,1,0:T(8,128)}) fusion(f32[8,2,7,128,128]{3,4,2,1,0:T(8,128)S(1)} %fusion.7, f32[8,2,7,128,128]{3,4,2,1,0:T(8,128)} %fusion.8), kind=kLoop, calls=%fused_computation.21 | loop fusion | flops 1835008 | bytes 22020096 | tf_op jit(solution)/shard_map/sub | solution.py:16
  222.7 2.6 fusion
  225.3 1.9 broadcast_in_dim.55
  227.2 4.5 %all-to-all-start.2 = ((bf16[32,2,128,128]{2,3,1,0:T(8,128)(2,1)}), bf16[32,2,128,128]{2,3,1,0:T(8,128)(2,1)S(1)}, u32[]{:S(2)}, u32[]{:S(2)}) async-start(bf16[32,2,128,128]{2,3,1,0:T(8,128)(2,1)} %bitcast.72), calls=%async_computation.2 | async-start | bytes 4194304 | tf_op jit(solution)/shard_map/all_to_all | solution.py:53
  231.6 6.1 %slice_bitcast_fusion.1 = (bf16[2,64,128,128]{3,2,1,0:T(8,128)(2,1)}, bf16[2,64,128,128]{3,2,1,0:T(8,128)(2,1)}) fusion(bf16[2,64,2,128,128]{4,3,2,1,0:T(8,128)(2,1)} %param.8), kind=kLoop, calls=%fused_computation.16 | loop fusion | bytes 16777216 | tf_op jit(solution)/shard_map/squeeze | solution.py:31
  237.7 22.6 %all-to-all-done.2 = bf16[32,2,128,128]{2,3,1,0:T(8,128)(2,1)S(1)} async-done(((bf16[32,2,128,128]{2,3,1,0:T(8,128)(2,1)}), bf16[32,2,128,128]{2,3,1,0:T(8,128)(2,1)S(1)}, u32[]{:S(2)}, u32[]{:S(2)}) %all-to-all-start.2) | async-done | bytes 2097184 | tf_op jit(solution)/shard_map/all_to_all | solution.py:53
  260.2 0.0 copy-start.5
  260.2 3.6 %fusion.11 = f32[2,64,128,128]{2,3,0,1:T(8,128)S(1)} fusion(bf16[64,128,128,1]{1,2,3,0:T(8,128)(2,1)S(1)} %bitcast.68, bf16[2,64,128,128]{3,2,1,0:T(8,128)(2,1)} %get-tuple-element.11), kind=kOutput, calls=%fused_computation.28 | convolution fusion | flops 536870912 | bytes 14680064 | tf_op jit(solution)/shard_map/cesr,esa->cera/dot_general | solution.py:12
  263.8 0.0 copy-done.5
  263.8 1.2 fusion.14
  265.1 2.1 slice_subtract_fusion
  267.2 2.3 pad_maximum_fusion
  269.5 0.0 copy-start.6
  269.5 0.0 copy-start.1
  269.5 6.7 %copy.44 = bf16[2,64,128,128]{3,1,2,0:T(8,128)(2,1)} copy(bf16[2,64,128,128]{2,3,0,1:T(8,128)(2,1)} %pad_maximum_fusion) | data formatting | bytes 8388608 | tf_op jit(solution)/shard_map/concatenate | solution.py:14
  276.1 0.0 copy-done.6
  276.1 2.8 %convolution_convert_fusion = bf16[2,16,128,128]{3,1,2,0:T(8,128)(2,1)S(1)} fusion(bf16[2,64,128,128]{3,1,2,0:T(8,128)(2,1)} %copy.44, s32[2,64]{1,0:T(2,128)S(1)} %copy-done.6), kind=kOutput, calls=%fused_computation.33 | convolution fusion | flops 67110912 | bytes 5243392 | tf_op jit(solution)/shard_map/cie,cera->cira/dot_general | solution.py:57
  279.0 1.2 copy.45
  280.2 0.0 copy-done.1
  (2 shorter events, 0.0 us)
Async XLA Ops:
  0.0 101.0 %copy-start = (bf16[2,8,2,128,128]{4,3,2,1,0:T(8,128)(2,1)S(1)}, bf16[2,8,2,128,128]{4,3,2,1,0:T(8,128)(2,1)}, u32[]{:S(2)}) copy-start(bf16[2,8,2,128,128]{4,3,2,1,0:T(8,128)(2,1)} %param.13) | copy-start | bytes 3145732
  12.2 9.9 %copy-start.2 = (bf16[2,64,128,128]{2,3,1,0:T(8,128)(2,1)S(1)}, bf16[2,64,128,128]{2,3,1,0:T(8,128)(2,1)}, u32[]{:S(2)}) copy-start(bf16[2,64,128,128]{2,3,1,0:T(8,128)(2,1)} %copy.35) | copy-start | bytes 12582916
  92.2 8.3 %copy-start.7 = (s32[8,2,7]{0,1,2:T(2,128)S(1)}, s32[8,2,7]{0,1,2:T(2,128)}, u32[]{:S(2)}) copy-start(s32[8,2,7]{0,1,2:T(2,128)} %param.10) | copy-start | bytes 1348
  92.2 8.6 %copy-start.8 = (s32[8,2,7]{0,1,2:T(2,128)S(1)}, s32[8,2,7]{0,1,2:T(2,128)}, u32[]{:S(2)}) copy-start(s32[8,2,7]{0,1,2:T(2,128)} %param.11) | copy-start | bytes 1348
  92.2 105.2 %all-to-all-start.1 = ((bf16[8,8,2,128,128]{4,3,2,1,0:T(8,128)(2,1)}), bf16[8,8,2,128,128]{4,3,2,1,0:T(8,128)(2,1)}, u32[]{:S(2)}, u32[]{:S(2)}) async-start(bf16[8,8,2,128,128]{4,3,2,1,0:T(8,128)(2,1)} %stack.2), calls=%async_computation.1 | async-start | bytes 8388608 | tf_op jit(solution)/shard_map/all_to_all | solution.py:38
  108.8 9.2 %copy-start.9 = (s32[8,2]{0,1:T(2,128)S(1)}, s32[8,2]{0,1:T(2,128)}, u32[]{:S(2)}) copy-start(s32[8,2]{0,1:T(2,128)} %param.12) | copy-start | bytes 196
  203.0 6.0 %copy-start.3 = (bf16[112,128,128]{2,1,0:T(8,128)(2,1)S(1)}, bf16[112,128,128]{2,1,0:T(8,128)(2,1)}, u32[]{:S(2)}) copy-start(bf16[112,128,128]{2,1,0:T(8,128)(2,1)} %gather_fusion.1) | copy-start | bytes 11010052
  203.0 6.3 %copy-start.4 = (bf16[112,2,128,128]{3,2,0,1:T(8,128)(2,1)S(1)}, bf16[112,2,128,128]{3,2,0,1:T(8,128)(2,1)}, u32[]{:S(2)}) copy-start(bf16[112,2,128,128]{3,2,0,1:T(8,128)(2,1)} %copy.34) | copy-start | bytes 22020100
  227.2 33.1 %all-to-all-start.2 = ((bf16[32,2,128,128]{2,3,1,0:T(8,128)(2,1)}), bf16[32,2,128,128]{2,3,1,0:T(8,128)(2,1)S(1)}, u32[]{:S(2)}, u32[]{:S(2)}) async-start(bf16[32,2,128,128]{2,3,1,0:T(8,128)(2,1)} %bitcast.72), calls=%async_computation.2 | async-start | bytes 4194304 | tf_op jit(solution)/shard_map/all_to_all | solution.py:53
  260.2 3.6 %copy-start.5 = (bf16[2,64,128,128]{3,2,1,0:T(8,128)(2,1)S(1)}, bf16[2,64,128,128]{3,2,1,0:T(8,128)(2,1)}, u32[]{:S(2)}) copy-start(bf16[2,64,128,128]{3,2,1,0:T(8,128)(2,1)} %get-tuple-element.12) | copy-start | bytes 12582916
  269.5 6.7 %copy-start.6 = (s32[2,64]{1,0:T(2,128)S(1)}, s32[2,64]{1,0:T(2,128)}, u32[]{:S(2)}) copy-start(s32[2,64]{1,0:T(2,128)} %param.9) | copy-start | bytes 1540
  269.5 10.8 %copy-start.1 = (bf16[2,8,2,128,128]{4,3,2,1,0:T(8,128)(2,1)S(1)}, bf16[2,8,2,128,128]{4,3,2,1,0:T(8,128)(2,1)}, u32[]{:S(2)}) copy-start(bf16[2,8,2,128,128]{4,3,2,1,0:T(8,128)(2,1)} %param.13) | copy-start | bytes 3145732
